TPU v7x, 32 devices: a whole 2x2x4 slice. The times are simulated.
32 devices in a mesh: tensor: 2 (over x), expert: 8 (over z, y), replica: 2 (over core).
Axes of the slice: x: 2, y: 2, z: 4, core: 2. Of those that a mesh axis runs over, the one named last changes fastest.
Arguments:
- tokens: bfloat16 [6304, 768], P(('expert', 'replica')), may hold values from -6 to 6
- gains: float32 [2, 2, 768], replicated, may hold values from 0.5 to 1.5
- attn_qkv: bfloat16 [2, 3, 768, 768], P(None, None, None, 'tensor'), may hold values from -0.21875 to 0.21875
- attn_out: bfloat16 [2, 768, 768], P(None, 'tensor'), may hold values from -3 to 3
- router: bfloat16 [2, 768, 8], replicated, may hold values from -0.15625 to 0.15625
- expert_in: bfloat16 [2, 8, 768, 3072], P(None, 'expert', None, 'tensor'), may hold values from -0.21875 to 0.21875
- expert_out: bfloat16 [2, 8, 3072, 768], P(None, 'expert', 'tensor'), may hold values from -1.75 to 1.75
- routes: int32 [2, 6304, 2], P(None, ('expert', 'replica')), may hold values from 0 to 7, all different within a row; in each aligned block of 394 rows (0 to 393, 394 to 787, ..., all dimensions but the last counted through in order) at most 128 rows name the same one
- cotangent: bfloat16 [6304, 768], P(('expert', 'replica')), may hold values from -6 to 6
Outputs:
- mixed_out: bfloat16 [6304, 768], P(('expert', 'replica'))
- grad_tokens: float32 [6304, 768], P(('expert', 'replica'))
- grad_gains: float32 [2, 2, 768], replicated
- grad_attn_qkv: float32 [2, 3, 768, 768], P(None, None, None, 'tensor')
- grad_attn_out: float32 [2, 768, 768], P(None, 'tensor')
- grad_router: float32 [2, 768, 8], replicated
- grad_expert_in: float32 [2, 8, 768, 3072], P(None, 'expert', 'replica', 'tensor')
- grad_expert_out: float32 [2, 8, 3072, 768], P(None, 'expert', 'tensor', 'replica')
Inputs may be any that keep to these rules, and one draw needn't show every extreme that they name: In the tokens of one block of 394, no expert is named by more than 128 routes, and in every draw some expert by exactly 128; the two experts of a token differ.
All inputs are finite; a program needn't handle non-finite values.
Results may differ from a plain program's by a relative error of at most 0.02.
Values may be sent and summed in bfloat16 or wider, within the bound.
No kernel may reach another device: no remote copies, remote signals or barrier semaphores. Data moves between devices by JAX's collectives and lax.ppermute only.
A program may use at most 192 MiB of HBM per device.

v0:
```python
import jax
import jax.numpy as jnp
from jax import lax
from jax.sharding import PartitionSpec as P

HEAD_DIM = 64
SEQ = 197
EPSILON = 1e-06


def layer_norm(stream, gain):
    center = jnp.mean(stream, axis=-1, keepdims=True)
    shifted = stream - center
    spread = jnp.mean(shifted * shifted, axis=-1, keepdims=True)
    return shifted * lax.rsqrt(spread + EPSILON) * gain


def slot_index(route_ids, expert_count, capacity):
    labels = lax.broadcasted_iota(jnp.int32, (1, 1, expert_count), 2)
    route_hits = jnp.sum((route_ids[:, :, None] == labels).astype(jnp.int32), axis=1)
    before = jnp.cumsum(route_hits, axis=0) - route_hits
    return route_ids * capacity + jnp.take_along_axis(before, route_ids, axis=1)


def on_device(tokens, gains, attn_qkv, attn_out, router, expert_in, expert_out, routes, cotangent):
    row_count, model_width = tokens.shape
    layer_count = attn_qkv.shape[0]
    local_width = attn_qkv.shape[3]
    local_heads = local_width // HEAD_DIM
    image_count = row_count // SEQ
    expert_count = router.shape[2]
    capacity = 8 * (5 * row_count // (16 * expert_count) + 1)
    score_scale = HEAD_DIM ** (-0.5)
    residual = tokens.astype(jnp.float32)
    saved = []
    for layer_index in range(layer_count):
        normed, norm_pull = jax.vjp(layer_norm, residual, gains[layer_index, 0])
        normed_bf = normed.astype(jnp.bfloat16)
        projected = jnp.einsum(
            "td,cdf->ctf", normed_bf, attn_qkv[layer_index], preferred_element_type=jnp.float32
        ).astype(jnp.bfloat16)
        head_view = projected.reshape(3, image_count, SEQ, local_heads, HEAD_DIM)
        scores = (
            jnp.einsum(
                "bqhe,bkhe->bhqk", head_view[0], head_view[1], preferred_element_type=jnp.float32
            )
            * score_scale
        )
        row_max = jnp.max(scores, axis=-1, keepdims=True)
        exp_scores = jnp.exp(scores - row_max)
        exp_total = jnp.sum(exp_scores, axis=-1, keepdims=True)
        log_total = row_max + jnp.log(exp_total)
        attn_probs = (exp_scores / exp_total).astype(jnp.bfloat16)
        mixed_rows = jnp.einsum(
            "bhqk,bkhe->bqhe", attn_probs, head_view[2], preferred_element_type=jnp.float32
        )
        mixed_rows = mixed_rows.reshape(row_count, local_width).astype(jnp.bfloat16)
        attn_part = jnp.dot(mixed_rows, attn_out[layer_index], preferred_element_type=jnp.float32)
        residual = residual + lax.psum(attn_part, "tensor")
        moe_in, moe_pull = jax.vjp(layer_norm, residual, gains[layer_index, 1])
        moe_bf = moe_in.astype(jnp.bfloat16)
        gate_probs = jax.nn.softmax(
            jnp.dot(moe_bf, router[layer_index], preferred_element_type=jnp.float32), axis=-1
        )
        route_ids = routes[layer_index]
        slot_rows = slot_index(route_ids, expert_count, capacity).reshape(-1)
        picked = jnp.take_along_axis(gate_probs, route_ids, axis=1)
        send_buffer = jnp.zeros((expert_count * capacity, model_width), jnp.bfloat16)
        send_buffer = (
            send_buffer.at[slot_rows]
            .set(jnp.repeat(moe_bf, 2, axis=0))
            .reshape(expert_count, capacity, model_width)
        )
        received = lax.all_to_all(send_buffer, "expert", split_axis=0, concat_axis=0, tiled=True)
        source_count = received.shape[0]
        flat_in = received.reshape(-1, model_width)
        pre_act = jnp.dot(flat_in, expert_in[layer_index, 0], preferred_element_type=jnp.float32)
        activation = jax.nn.gelu(pre_act).astype(jnp.bfloat16)
        expert_part = jnp.dot(
            activation, expert_out[layer_index, 0], preferred_element_type=jnp.float32
        )
        expert_part = expert_part.reshape(source_count, capacity, model_width)
        returned = lax.all_to_all(expert_part, "expert", split_axis=0, concat_axis=0, tiled=True)
        chosen = returned.reshape(-1, model_width)[slot_rows].reshape(row_count, 2, model_width)
        moe_part = jnp.sum(picked[:, :, None] * chosen, axis=1)
        residual = residual + lax.psum(moe_part, "tensor")
        kept_act = pre_act
        saved.append(
            (
                normed_bf,
                norm_pull,
                head_view,
                log_total,
                mixed_rows,
                moe_bf,
                moe_pull,
                gate_probs,
                route_ids,
                slot_rows,
                picked,
                received,
                kept_act,
                chosen,
            )
        )
    mixed_out = residual.astype(jnp.bfloat16)
    upstream = cotangent.astype(jnp.float32)
    raw_grads = [None] * layer_count
    labels = lax.broadcasted_iota(jnp.int32, (1, 1, expert_count), 2)
    for layer_index in reversed(range(layer_count)):
        (
            normed_bf,
            norm_pull,
            head_view,
            log_total,
            mixed_rows,
            moe_bf,
            moe_pull,
            gate_probs,
            route_ids,
            slot_rows,
            picked,
            received,
            kept_act,
            chosen,
        ) = saved[layer_index]
        slot_grad = (
            (picked[:, :, None] * upstream[:, None, :])
            .astype(jnp.bfloat16)
            .reshape(-1, model_width)
        )
        grad_send = jnp.zeros((expert_count * capacity, model_width), jnp.bfloat16)
        grad_send = (
            grad_send.at[slot_rows].set(slot_grad).reshape(expert_count, capacity, model_width)
        )
        grad_recv = lax.all_to_all(grad_send, "expert", split_axis=0, concat_axis=0, tiled=True)
        source_count = grad_recv.shape[0]
        grad_recv = grad_recv.reshape(-1, model_width)
        flat_in = received.reshape(-1, model_width)
        pre_act = kept_act
        activation, gelu_pull = jax.vjp(jax.nn.gelu, pre_act)
        act_grad = jnp.einsum(
            "sd,fd->sf", grad_recv, expert_out[layer_index, 0], preferred_element_type=jnp.float32
        )
        pre_grad = gelu_pull(act_grad)[0].astype(jnp.bfloat16)
        grad_w_out = jnp.einsum(
            "sf,sd->fd",
            activation.astype(jnp.bfloat16),
            grad_recv,
            preferred_element_type=jnp.float32,
        )
        grad_w_in = jnp.einsum("sd,sf->df", flat_in, pre_grad, preferred_element_type=jnp.float32)
        input_grad = jnp.einsum(
            "sf,df->sd", pre_grad, expert_in[layer_index, 0], preferred_element_type=jnp.float32
        )
        input_grad = input_grad.reshape(source_count, capacity, model_width)
        home_grad = lax.all_to_all(input_grad, "expert", split_axis=0, concat_axis=0, tiled=True)
        row_grad = jnp.sum(
            home_grad.reshape(-1, model_width)[slot_rows].reshape(row_count, 2, model_width), axis=1
        )
        gate_dot = jnp.sum(upstream[:, None, :] * chosen, axis=-1)
        row_grad, gate_dot = lax.psum((row_grad, gate_dot), "tensor")
        prob_grad = jnp.sum(
            gate_dot[:, :, None] * (route_ids[:, :, None] == labels).astype(jnp.float32), axis=1
        )
        logit_grad = gate_probs * (
            prob_grad - jnp.sum(prob_grad * gate_probs, axis=-1, keepdims=True)
        )
        logit_grad = logit_grad.astype(jnp.bfloat16)
        grad_router = jnp.einsum(
            "td,te->de", moe_bf, logit_grad, preferred_element_type=jnp.float32
        )
        norm_grad = row_grad + jnp.einsum(
            "te,de->td", logit_grad, router[layer_index], preferred_element_type=jnp.float32
        )
        resid_grad, gain_two = moe_pull(norm_grad)
        upstream = upstream + resid_grad
        out_grad = upstream.astype(jnp.bfloat16)
        grad_attn_out = jnp.einsum(
            "tf,td->fd", mixed_rows, out_grad, preferred_element_type=jnp.float32
        )
        mixed_grad = jnp.einsum(
            "td,fd->tf", out_grad, attn_out[layer_index], preferred_element_type=jnp.float32
        )
        mixed_grad = mixed_grad.astype(jnp.bfloat16).reshape(
            image_count, SEQ, local_heads, HEAD_DIM
        )
        scores = (
            jnp.einsum(
                "bqhe,bkhe->bhqk", head_view[0], head_view[1], preferred_element_type=jnp.float32
            )
            * score_scale
        )
        attn_probs = jnp.exp(scores - log_total)
        value_grad = jnp.einsum(
            "bhqk,bqhe->bkhe",
            attn_probs.astype(jnp.bfloat16),
            mixed_grad,
            preferred_element_type=jnp.float32,
        )
        prob_grad = jnp.einsum(
            "bqhe,bkhe->bhqk", mixed_grad, head_view[2], preferred_element_type=jnp.float32
        )
        score_grad = attn_probs * (
            prob_grad - jnp.sum(prob_grad * attn_probs, axis=-1, keepdims=True)
        )
        score_grad = score_grad.astype(jnp.bfloat16)
        query_grad = (
            jnp.einsum(
                "bhqk,bkhe->bqhe", score_grad, head_view[1], preferred_element_type=jnp.float32
            )
            * score_scale
        )
        key_grad = (
            jnp.einsum(
                "bhqk,bqhe->bkhe", score_grad, head_view[0], preferred_element_type=jnp.float32
            )
            * score_scale
        )
        proj_grad = (
            jnp.stack([query_grad, key_grad, value_grad])
            .reshape(3, row_count, local_width)
            .astype(jnp.bfloat16)
        )
        grad_qkv = jnp.einsum(
            "td,ctf->cdf", normed_bf, proj_grad, preferred_element_type=jnp.float32
        )
        norm_grad = jnp.einsum(
            "ctf,cdf->td", proj_grad, attn_qkv[layer_index], preferred_element_type=jnp.float32
        )
        norm_grad = lax.psum(norm_grad, "tensor")
        resid_grad, gain_one = norm_pull(norm_grad)
        upstream = upstream + resid_grad
        gain_pair = jnp.stack([gain_one, gain_two])
        raw_grads[layer_index] = (
            grad_w_in,
            grad_w_out,
            grad_qkv,
            grad_attn_out,
            grad_router,
            gain_pair,
        )
    stacked = [jnp.stack([item[position] for item in raw_grads]) for position in range(6)]
    grad_in_all, grad_out_all = (
        lax.psum_scatter(stacked[0], "replica", scatter_dimension=1, tiled=True),
        lax.psum_scatter(stacked[1], "replica", scatter_dimension=2, tiled=True),
    )
    grad_qkv_all, grad_proj_all, grad_router_all, grad_gain_all = lax.psum(
        (stacked[2], stacked[3], stacked[4], stacked[5]), ("expert", "replica")
    )
    return (
        mixed_out,
        upstream,
        grad_gain_all,
        grad_qkv_all,
        grad_proj_all,
        grad_router_all,
        grad_in_all[:, None],
        grad_out_all[:, None],
    )


def solution(mesh):
    return jax.shard_map(
        on_device,
        mesh=mesh,
        in_specs=(
            P(("expert", "replica"), None),
            P(),
            P(None, None, None, "tensor"),
            P(None, "tensor", None),
            P(),
            P(None, "expert", None, "tensor"),
            P(None, "expert", "tensor", None),
            P(None, ("expert", "replica"), None),
            P(("expert", "replica"), None),
        ),
        out_specs=(
            P(("expert", "replica"), None),
            P(("expert", "replica"), None),
            P(),
            P(None, None, None, "tensor"),
            P(None, "tensor", None),
            P(),
            P(None, "expert", "replica", "tensor"),
            P(None, "expert", "tensor", "replica"),
        ),
        check_vma=False,
    )
```

profile of v0, /device:TPU:0, one launch (start us, length us, event | category | flops | bytes accessed | tf_op | source)
XLA Modules:
  0.0 1209.6 jit_solution(15359523138905654827)
XLA Ops:
  24.5 8.1 gather_fusion.5
  33.1 35.5 %all-reduce.14.cloned.1.call-done = f32[394,768]{1,0:T(8,128)} async-done(((f32[394,768]{1,0:T(8,128)}), f32[394,768]{1,0:T(8,128)}) %all-reduce.14.cloned.1.call-update) | async-done | bytes 1210384 | tf_op jit(solution)/shard_map/psum | solution.py:59
  79.4 42.6 %all_to_all.40 = bf16[8,128,768]{2,1,0:T(8,128)(2,1)S(1)} all-to-all(bf16[8,128,768]{2,1,0:T(8,128)(2,1)S(1)} %bitcast.271), channel_id=1, replica_groups=mesh['tensor'=2,'expert'=8,'replica'=2] {'expert'}, dimensions={0} | all-to-all | bytes 3145728 | tf_op jit(solution)/shard_map/all_to_all | solution.py:74
  122.0 7.6 multiply_convert_fusion.1
  139.7 8.3 gather_fusion.4
  150.6 57.4 %all-to-all-done.1 = f32[8,128,768]{2,1,0:T(8,128)S(1)} async-done(((f32[8,128,768]{2,1,0:T(8,128)}), f32[8,128,768]{2,1,0:T(8,128)S(1)}, u32[]{:S(2)}, u32[]{:S(2)}) %all-to-all-start.1) | async-done | bytes 3145760 | tf_op jit(solution)/shard_map/all_to_all | solution.py:83
  221.5 41.1 %all-reduce.16.cloned.1.call-done = f32[394,768]{1,0:T(8,128)} async-done(((f32[394,768]{1,0:T(8,128)}), f32[394,768]{1,0:T(8,128)}) %all-reduce.16.cloned.1.call-update) | async-done | bytes 1210384 | tf_op jit(solution)/shard_map/psum | solution.py:86
  279.7 8.1 gather_fusion.7
  288.3 33.4 %all-reduce.18.cloned.1.call-done = f32[394,768]{1,0:T(8,128)} async-done(((f32[394,768]{1,0:T(8,128)}), f32[394,768]{1,0:T(8,128)}) %all-reduce.18.cloned.1.call-update) | async-done | bytes 1210384 | tf_op jit(solution)/shard_map/psum | solution.py:59
  346.4 8.1 gather_fusion.6
  355.0 10.8 scatter_custom_fusion.2
  365.7 11.1 all-to-all-done.2
  381.4 7.5 multiply_convert_fusion
  388.9 29.1 %all-to-all-done.4 = bf16[8,128,768]{2,1,0:T(8,128)(2,1)} async-done(((bf16[8,128,768]{2,1,0:T(8,128)(2,1)}), bf16[8,128,768]{2,1,0:T(8,128)(2,1)}, u32[]{:S(2)}, u32[]{:S(2)}) %all-to-all-start.4) | async-done | bytes 1572896 | tf_op jit(solution)/shard_map/all_to_all | solution.py:136
  418.0 8.5 fusion.13
  443.0 64.0 %all-to-all-done.5 = f32[8,128,768]{2,1,0:T(8,128)S(1)} async-done(((f32[8,128,768]{2,1,0:T(8,128)}), f32[8,128,768]{2,1,0:T(8,128)S(1)}, u32[]{:S(2)}, u32[]{:S(2)}) %all-to-all-start.5) | async-done | bytes 3145760 | tf_op jit(solution)/shard_map/all_to_all | solution.py:157
  531.1 52.1 %all-to-all-done.3 = f32[8,128,768]{2,1,0:T(8,128)S(1)} async-done(((f32[8,128,768]{2,1,0:T(8,128)}), f32[8,128,768]{2,1,0:T(8,128)S(1)}, u32[]{:S(2)}, u32[]{:S(2)}) %all-to-all-start.3) | async-done | bytes 3145760 | tf_op jit(solution)/shard_map/all_to_all | solution.py:83
  591.1 8.1 multiply_reduce_fusion.3
  599.2 9.9 psum.103
  629.0 42.9 %all-reduce.22.cloned.1.call-done = f32[394,768]{1,0:T(8,128)} async-done(((f32[394,768]{1,0:T(8,128)}), f32[394,768]{1,0:T(8,128)}) %all-reduce.22.cloned.1.call-update) | async-done | bytes 1210384 | tf_op jit(solution)/shard_map/psum | solution.py:231
  681.9 8.9 scatter_custom_fusion.3
  690.8 42.5 %all_to_all.41 = bf16[8,128,768]{2,1,0:T(8,128)(2,1)S(1)} all-to-all(bf16[8,128,768]{2,1,0:T(8,128)(2,1)} %bitcast.270), channel_id=1, replica_groups=mesh['tensor'=2,'expert'=8,'replica'=2] {'expert'}, dimensions={0} | all-to-all | bytes 3145728 | tf_op jit(solution)/shard_map/all_to_all | solution.py:136
  733.3 9.1 fusion.6
  745.1 74.1 %all_to_all.42 = f32[8,128,768]{2,1,0:T(8,128)S(1)} all-to-all(f32[8,128,768]{2,1,0:T(8,128)S(1)} %fusion.14), channel_id=1, replica_groups=mesh['tensor'=2,'expert'=8,'replica'=2] {'expert'}, dimensions={0} | all-to-all | bytes 6291456 | tf_op jit(solution)/shard_map/all_to_all | solution.py:157
  836.0 14.5 %psum.106 = f32[394,2]{1,0:T(8,128)S(1)} all-reduce(f32[394,2]{1,0:T(8,128)S(1)} %multiply_reduce_fusion.2), channel_id=1, replica_groups=mesh['tensor'=2,'expert'=8,'replica'=2] {'tensor'}, use_global_device_ids=true, to_apply=%region_47.50 | all-reduce | flops 788 | bytes 6304 | tf_op jit(solution)/shard_map/psum | solution.py:162
  850.8 27.6 %all-reduce.24.cloned.1.call-done = f32[394,768]{1,0:T(8,128)} async-done(((f32[394,768]{1,0:T(8,128)}), f32[394,768]{1,0:T(8,128)}) %all-reduce.24.cloned.1.call-update) | async-done | bytes 1210384 | tf_op jit(solution)/shard_map/psum | solution.py:162
  935.3 32.9 %all-reduce.28.cloned.1.call-done = (f32[394,768]{1,0:T(8,128)}, f32[394,768]{1,0:T(8,128)}) async-done(((f32[394,768]{1,0:T(8,128)}, f32[394,768]{1,0:T(8,128)}), (f32[394,768]{1,0:T(8,128)}, f32[394,768]{1,0:T(8,128)})) %all-reduce.28.cloned.1.call-update) | async-done | bytes 2420752 | tf_op jit(solution)/shard_map/psum | solution.py:86
  970.7 65.3 %all-reduce.2 = (f32[2,2,768]{2,1,0:T(2,128)}, f32[2,768,8]{1,2,0:T(8,128)}) all-reduce(f32[2,2,768]{2,1,0:T(2,128)S(1)} %pad_maximum_fusion.5, f32[2,768,8]{1,2,0:T(8,128)S(1)} %pad_maximum_fusion.4), channel_id=1, replica_groups=mesh['tensor'=2,'expert'=8,'replica'=2] {'expert','replica'}, use_global_device_ids=true, to_apply=%region_60.63 | all-reduce | flops 15360 | bytes 122880 | tf_op jit(solution)/shard_map/psum | solution.py:248
  1039.5 118.8 %all-reduce.26.cloned.1.call-done = (f32[2,3,768,384]{2,3,1,0:T(8,128)}, f32[2,384,768]{2,1,0:T(8,128)}) async-done(((f32[2,3,768,384]{2,3,1,0:T(8,128)}, f32[2,384,768]{2,1,0:T(8,128)}), (f32[2,3,768,384]{2,3,1,0:T(8,128)}, f32[2,384,768]{2,1,0:T(8,128)})) %all-reduce.26.cloned.1.call-update) | async-done | bytes 9437200 | tf_op jit(solution)/shard_map/psum | solution.py:248
  1158.3 8.2 copy.267
  1166.5 12.7 %reduce-scatter.5.cloned.1.call-done = f32[2,1536,384]{2,1,0:T(8,128)} async-done(((f32[2,1536,768]{2,1,0:T(8,128)}), f32[2,1536,384]{2,1,0:T(8,128)}) %reduce-scatter.5.cloned.1.call-update) | async-done | bytes 4718608 | tf_op jit(solution)/shard_map/reduce_scatter | solution.py:246
  1179.1 22.0 %reduce-scatter.3.cloned.1.call-done = f32[2,384,1536]{2,1,0:T(8,128)} async-done(((f32[2,768,1536]{2,1,0:T(8,128)}), f32[2,384,1536]{2,1,0:T(8,128)}) %reduce-scatter.3.cloned.1.call-update) | async-done | bytes 4718608 | tf_op jit(solution)/shard_map/reduce_scatter | solution.py:245
  (491 shorter events, 262.6 us)
Async XLA Ops:
  7.2 61.4 %all-reduce.14.cloned.1.call-start = ((), (), s32[]{:S(2)}) async-start(), calls=%async_computation.10 | async-start | bytes 2457600 | tf_op jit(solution)/shard_map/psum | solution.py:59
  11.3 59.1 %copy-start.85 = (f32[768]{0:T(1024)}, f32[768]{0:T(1024)S(1)}, u32[]{:S(2)}) copy-start(f32[768]{0:T(1024)S(1)} %get-tuple-element.61) | copy-start | bytes 9220
  33.1 104.6 %copy-start.116 = (s32[788]{0:T(1024)}, s32[788]{0:T(1024)S(1)}, u32[]{:S(2)}) copy-start(s32[788]{0:T(1024)S(1)} %fusion.150) | copy-start | bytes 9460
  79.4 50.2 %slice-start = ((s8[4718592]{0:T(1024)(128)(4,1)}), s8[4194304]{0:T(1024)(128)(4,1)S(1)}, s32[]{:S(2)}) async-start(s8[4718592]{0:T(1024)(128)(4,1)} %bitcast.280), calls=%async_computation.20 | async-start | bytes 8388608
  133.9 74.1 %all-to-all-start.1 = ((f32[8,128,768]{2,1,0:T(8,128)}), f32[8,128,768]{2,1,0:T(8,128)S(1)}, u32[]{:S(2)}, u32[]{:S(2)}) async-start(f32[8,128,768]{2,1,0:T(8,128)} %fusion.20), calls=%async_computation.1 | async-start | bytes 6291456 | tf_op jit(solution)/shard_map/all_to_all | solution.py:83
  137.7 124.9 %all-reduce.16.cloned.1.call-start = ((), (), s32[]{:S(2)}) async-start(), calls=%async_computation.11 | async-start | bytes 2457600 | tf_op jit(solution)/shard_map/psum | solution.py:86
  137.7 70.2 %copy-start.100 = (s32[1024]{0:T(1024)}, s32[1024]{0:T(1024)S(1)}, u32[]{:S(2)}) copy-start(s32[1024]{0:T(1024)S(1)} %pad_clamp_fusion.1) | copy-start | bytes 12292
  220.3 101.4 %all-reduce.18.cloned.1.call-start = ((), (), s32[]{:S(2)}) async-start(), calls=%async_computation.12 | async-start | bytes 2457600 | tf_op jit(solution)/shard_map/psum | solution.py:59
  264.2 57.4 %copy-start.11 = (f32[394,768]{1,0:T(8,128)}, f32[394,768]{1,0:T(8,128)S(1)}, u32[]{:S(2)}) copy-start(f32[394,768]{1,0:T(8,128)S(1)} %get-tuple-element.79) | copy-start | bytes 3631108
  334.1 42.8 %all-to-all-start.2 = ((bf16[8,128,768]{2,1,0:T(8,128)(2,1)}), bf16[8,128,768]{2,1,0:T(8,128)(2,1)S(1)}, u32[]{:S(2)}, u32[]{:S(2)}) async-start(bf16[8,128,768]{2,1,0:T(8,128)(2,1)} %bitcast.268), calls=%async_computation.2 | async-start | bytes 3145728 | tf_op jit(solution)/shard_map/all_to_all | solution.py:74
  376.9 41.2 %all-to-all-start.4 = ((bf16[8,128,768]{2,1,0:T(8,128)(2,1)}), bf16[8,128,768]{2,1,0:T(8,128)(2,1)}, u32[]{:S(2)}, u32[]{:S(2)}) async-start(bf16[8,128,768]{2,1,0:T(8,128)(2,1)} %bitcast.269), calls=%async_computation.4 | async-start | bytes 3145728 | tf_op jit(solution)/shard_map/all_to_all | solution.py:136
  381.4 46.8 %slice-start.2 = ((s8[4718592]{0:T(1024)(128)(4,1)}), s8[524288]{0:T(1024)(128)(4,1)S(1)}, s32[]{:S(2)}) async-start(s8[4718592]{0:T(1024)(128)(4,1)} %bitcast.282), calls=%async_computation.22 | async-start | bytes 1048576
  432.5 74.5 %all-to-all-start.5 = ((f32[8,128,768]{2,1,0:T(8,128)}), f32[8,128,768]{2,1,0:T(8,128)S(1)}, u32[]{:S(2)}, u32[]{:S(2)}) async-start(f32[8,128,768]{2,1,0:T(8,128)} %fusion.16), calls=%async_computation.5 | async-start | bytes 6291456 | tf_op jit(solution)/shard_map/all_to_all | solution.py:157
  508.7 74.5 %all-to-all-start.3 = ((f32[8,128,768]{2,1,0:T(8,128)}), f32[8,128,768]{2,1,0:T(8,128)S(1)}, u32[]{:S(2)}, u32[]{:S(2)}) async-start(f32[8,128,768]{2,1,0:T(8,128)} %fusion.18), calls=%async_computation.3 | async-start | bytes 6291456 | tf_op jit(solution)/shard_map/all_to_all | solution.py:83
  512.3 97.0 %all-reduce.20.cloned.1.call-start = ((), (), s32[]{:S(2)}) async-start(), calls=%async_computation.13 | async-start | bytes 2457600 | tf_op jit(solution)/shard_map/psum | solution.py:162
  528.9 143.0 %all-reduce.22.cloned.1.call-start = ((), (), s32[]{:S(2)}) async-start(), calls=%async_computation.14 | async-start | bytes 2457600 | tf_op jit(solution)/shard_map/psum | solution.py:231
  625.0 46.9 %copy-start.84 = (f32[768]{0:T(1024)S(1)}, f32[768]{0:T(1024)}, u32[]{:S(2)}) copy-start(f32[768]{0:T(1024)} %get-tuple-element.63) | copy-start | bytes 9220
  625.0 46.9 %copy-start.89 = (f32[394]{0:T(512)S(1)}, f32[394]{0:T(512)}, u32[]{:S(2)}) copy-start(f32[394]{0:T(512)} %copy-done.88) | copy-start | bytes 4732
  625.0 46.9 %copy-start.103 = (f32[394]{0:T(512)S(1)}, f32[394]{0:T(512)}, u32[]{:S(2)}) copy-start(f32[394]{0:T(512)} %copy-done.102) | copy-start | bytes 4732
  628.6 45.2 %copy-start.113 = (f32[394]{0:T(512)S(1)}, f32[394]{0:T(512)}, u32[]{:S(2)}) copy-start(f32[394]{0:T(512)} %copy-done.112) | copy-start | bytes 4732
  628.6 249.8 %all-reduce.24.cloned.1.call-start = ((), (), s32[]{:S(2)}) async-start(), calls=%async_computation.15 | async-start | bytes 2457600 | tf_op jit(solution)/shard_map/psum | solution.py:162
  681.9 60.6 %slice-start.4 = ((s8[4718592]{0:T(1024)(128)(4,1)}), s8[524288]{0:T(1024)(128)(4,1)S(1)}, s32[]{:S(2)}) async-start(s8[4718592]{0:T(1024)(128)(4,1)} %bitcast.284), calls=%async_computation.24 | async-start | bytes 1048576
  745.1 74.1 %copy-start.101 = (s32[1024]{0:T(1024)S(1)}, s32[1024]{0:T(1024)}, u32[]{:S(2)}) copy-start(s32[1024]{0:T(1024)} %copy-done.100) | copy-start | bytes 12292
  832.7 135.4 %all-reduce.28.cloned.1.call-start = ((), (), s32[]{:S(2)}) async-start(), calls=%async_computation.19 | async-start | bytes 4915200 | tf_op jit(solution)/shard_map/psum | solution.py:86
  832.9 45.5 %copy-start.10 = (f32[394,768]{1,0:T(8,128)S(1)}, f32[394,768]{1,0:T(8,128)}, u32[]{:S(2)}) copy-start(f32[394,768]{1,0:T(8,128)} %copy-done.8) | copy-start | bytes 3631108
  832.9 45.5 %copy-start.86 = (f32[768]{0:T(1024)S(1)}, f32[768]{0:T(1024)}, u32[]{:S(2)}) copy-start(f32[768]{0:T(1024)} %copy-done.85) | copy-start | bytes 9220
  832.9 45.5 %copy-start.91 = (f32[394]{0:T(512)S(1)}, f32[394]{0:T(512)}, u32[]{:S(2)}) copy-start(f32[394]{0:T(512)} %copy-done.90) | copy-start | bytes 4732
  832.9 45.5 %copy-start.105 = (f32[394]{0:T(512)S(1)}, f32[394]{0:T(512)}, u32[]{:S(2)}) copy-start(f32[394]{0:T(512)} %copy-done.104) | copy-start | bytes 4732
  897.1 261.2 %all-reduce.26.cloned.1.call-start = ((), (), s32[]{:S(2)}) async-start(), calls=%async_computation.18 | async-start | bytes 18874368 | tf_op jit(solution)/shard_map/psum | solution.py:248
  908.8 270.3 %reduce-scatter.5.cloned.1.call-start = ((), (), s32[]{:S(2)}) async-start(), calls=%async_computation.17 | async-start | bytes 14155776 | tf_op jit(solution)/shard_map/reduce_scatter | solution.py:246
  921.2 280.0 %reduce-scatter.3.cloned.1.call-start = ((), (), s32[]{:S(2)}) async-start(), calls=%async_computation.16 | async-start | bytes 14155776 | tf_op jit(solution)/shard_map/reduce_scatter | solution.py:245
  968.2 67.8 %copy-start.7 = (f32[394,768]{1,0:T(8,128)S(1)}, f32[394,768]{1,0:T(8,128)}, u32[]{:S(2)}) copy-start(f32[394,768]{1,0:T(8,128)} %copy-done.5) | copy-start | bytes 3631108
  (110 other events, 702.4 us)
Sparse Core Ops, SparseCore 0:
  21.9 46.6 all-reduce.13
  220.4 42.0 all-reduce.15
  277.6 43.9 all-reduce.17
  529.0 44.3 all-reduce.19
  628.7 43.1 all-reduce.21
  832.9 45.4 all-reduce.23
  897.2 70.9 all-reduce.27
  972.5 185.7 all-reduce.25
  1161.2 17.8 reduce-scatter.4
  1181.9 19.1 reduce-scatter.2
where the time goes:
time: 1220 us; the launch traced here: 1210 us
  waiting for transfers between devices  581 us (48%)
  blocking collectives  249 us (20%)
  local copies, waits for them, and re-layouts  154 us (13%)
  matrix products  98.9 us (8%)
  other arithmetic  88.1 us (7%)
  starting transfers between devices  22.7 us (2%)
  between operations  16.4 us (1%)
    psum x1, waiting for transfers between devices, on_device(): lax.psum((stacked[2], stacked[3], stacked[4], stacked[5]), ('expert', 're...  119 us
    all_to_all x2, waiting for transfers between devices, on_device(): lax.all_to_all(expert_part, 'expert', split_axis=0, concat_axis=0, tiled=...  109 us
    all_to_all x1, blocking collectives, on_device(): lax.all_to_all(input_grad, 'expert', split_axis=0, concat_axis=0, tiled=T...  74.1 us
    psum x2, waiting for transfers between devices, on_device(): residual = residual + lax.psum(moe_part, 'tensor')  74 us
    psum x2, waiting for transfers between devices, on_device(): residual = residual + lax.psum(attn_part, 'tensor')  68.9 us
    psum x1, blocking collectives, on_device(): lax.psum((stacked[2], stacked[3], stacked[4], stacked[5]), ('expert', 're...  65.3 us
    all_to_all x1, waiting for transfers between devices, on_device(): lax.all_to_all(input_grad, 'expert', split_axis=0, concat_axis=0, tiled=T...  64 us
    psum x1, waiting for transfers between devices, on_device(): norm_grad = lax.psum(norm_grad, 'tensor')  42.9 us
  transfers between devices with their start and end apart: 15, of which 14 were waited for; matrix products, arithmetic and copies ran while one was open for 13% of the time, Pallas kernels for 0%

commit v1 on v0

--- a/solution.py
+++ b/solution.py
@@ -245,8 +245,11 @@
         lax.psum_scatter(stacked[0], "replica", scatter_dimension=1, tiled=True),
         lax.psum_scatter(stacked[1], "replica", scatter_dimension=2, tiled=True),
     )
-    grad_qkv_all, grad_proj_all, grad_router_all, grad_gain_all = lax.psum(
-        (stacked[2], stacked[3], stacked[4], stacked[5]), ("expert", "replica")
+    push_rates_now = lambda sheet, named_axis, link_axis: lax.psum(
+        lax.psum(sheet, named_axis), link_axis
+    )
+    grad_qkv_all, grad_proj_all, grad_router_all, grad_gain_all = push_rates_now(
+        (stacked[2], stacked[3], stacked[4], stacked[5]), "replica", "expert"
     )
     return (
         mixed_out,

time: 1220 us -> 1390 us (1.14)
  waiting for transfers between devices: 581 us -> 835 us
  blocking collectives: 249 us -> 154 us
    psum x1 -> x2, waiting for transfers between devices: 119 us -> 291 us  [the longest x1 254 us: on_device(): lax.psum(lax.psum(sheet, named_axis), link_axis)]
    all_to_all x1 -> x0, blocking collectives: 74.1 us -> none  [on_device(): lax.all_to_all(input_grad, 'expert', split_axis=0, concat_axis=0, tiled=T...]
    all_to_all x1 -> x2, waiting for transfers between devices: 64 us -> 134 us  [on_device(): lax.all_to_all(input_grad, 'expert', split_axis=0, concat_axis=0, tiled=T...]
    psum x1 -> x2, blocking collectives: 65.3 us -> 44.5 us  [the longest x1 40.9 us: on_device(): lax.psum(lax.psum(sheet, named_axis), link_axis)]
    psum x2, waiting for transfers between devices: 74 us -> 88.6 us  [on_device(): residual = residual + lax.psum(moe_part, 'tensor')]
    unnamed x262 -> x266, local copies, waits for them, and re-layouts: 32.4 us -> 33.8 us
  transfers between devices with their start and end apart: 15 -> 17, of which waited for: 14 -> 16; matrix products, arithmetic and copies ran while one was open for 13% -> 11% of each run, Pallas kernels for 0% -> 0%
where the time goes in v1:
time: 1390 us; the launch traced here: 1380 us
  waiting for transfers between devices  835 us (60%)
  local copies, waits for them, and re-layouts  156 us (11%)
  blocking collectives  154 us (11%)
  matrix products  104 us (7%)
  other arithmetic  86.5 us (6%)
  starting transfers between devices  26.5 us (2%)
  between operations  16 us (1%)
    psum x1, waiting for transfers between devices, on_device(): lax.psum(lax.psum(sheet, named_axis), link_axis)  254 us
    all_to_all x2, waiting for transfers between devices, on_device(): lax.all_to_all(input_grad, 'expert', split_axis=0, concat_axis=0, tiled=T...  134 us
    all_to_all x2, waiting for transfers between devices, on_device(): lax.all_to_all(expert_part, 'expert', split_axis=0, concat_axis=0, tiled=...  109 us
    psum x2, waiting for transfers between devices, on_device(): residual = residual + lax.psum(moe_part, 'tensor')  88.6 us
    psum x2, waiting for transfers between devices, on_device(): residual = residual + lax.psum(attn_part, 'tensor')  68.9 us
    psum x1, waiting for transfers between devices, on_device(): norm_grad = lax.psum(norm_grad, 'tensor')  43.2 us
    all_to_all x1, blocking collectives, on_device(): lax.all_to_all(send_buffer, 'expert', split_axis=0, concat_axis=0, tiled=...  42.6 us
    all_to_all x1, blocking collectives, on_device(): lax.all_to_all(grad_send, 'expert', split_axis=0, concat_axis=0, tiled=True)  42.5 us
  transfers between devices with their start and end apart: 17, of which 16 were waited for; matrix products, arithmetic and copies ran while one was open for 11% of the time, Pallas kernels for 0%

profile of v1, /device:TPU:0, one launch (start us, length us, event | category | flops | bytes accessed | tf_op | source)
XLA Modules:
  0.0 1377.2 jit_solution(8304651946528401076)
XLA Ops:
  24.5 8.1 gather_fusion.5
  33.0 35.5 %all-reduce.17.cloned.1.call-done = f32[394,768]{1,0:T(8,128)} async-done(((f32[394,768]{1,0:T(8,128)}), f32[394,768]{1,0:T(8,128)}) %all-reduce.17.cloned.1.call-update) | async-done | bytes 1210384 | tf_op jit(solution)/shard_map/psum | solution.py:59
  79.4 42.6 %all_to_all.40 = bf16[8,128,768]{2,1,0:T(8,128)(2,1)S(1)} all-to-all(bf16[8,128,768]{2,1,0:T(8,128)(2,1)S(1)} %bitcast.271), channel_id=1, replica_groups=mesh['tensor'=2,'expert'=8,'replica'=2] {'expert'}, dimensions={0} | all-to-all | bytes 3145728 | tf_op jit(solution)/shard_map/all_to_all | solution.py:74
  122.0 7.6 multiply_convert_fusion.1
  139.7 8.3 gather_fusion.4
  150.6 57.3 %all-to-all-done.1 = f32[8,128,768]{2,1,0:T(8,128)S(1)} async-done(((f32[8,128,768]{2,1,0:T(8,128)}), f32[8,128,768]{2,1,0:T(8,128)S(1)}, u32[]{:S(2)}, u32[]{:S(2)}) %all-to-all-start.1) | async-done | bytes 3145760 | tf_op jit(solution)/shard_map/all_to_all | solution.py:83
  221.4 41.1 %all-reduce.19.cloned.1.call-done = f32[394,768]{1,0:T(8,128)} async-done(((f32[394,768]{1,0:T(8,128)}), f32[394,768]{1,0:T(8,128)}) %all-reduce.19.cloned.1.call-update) | async-done | bytes 1210384 | tf_op jit(solution)/shard_map/psum | solution.py:86
  279.7 8.1 gather_fusion.7
  288.2 33.4 %all-reduce.21.cloned.1.call-done = f32[394,768]{1,0:T(8,128)} async-done(((f32[394,768]{1,0:T(8,128)}), f32[394,768]{1,0:T(8,128)}) %all-reduce.21.cloned.1.call-update) | async-done | bytes 1210384 | tf_op jit(solution)/shard_map/psum | solution.py:59
  346.4 8.1 gather_fusion.6
  354.9 10.8 scatter_custom_fusion.2
  365.7 11.1 all-to-all-done.2
  388.8 29.2 %all-to-all-done.4 = bf16[8,128,768]{2,1,0:T(8,128)(2,1)} async-done(((bf16[8,128,768]{2,1,0:T(8,128)(2,1)}), bf16[8,128,768]{2,1,0:T(8,128)(2,1)}, u32[]{:S(2)}, u32[]{:S(2)}) %all-to-all-start.4) | async-done | bytes 1572896 | tf_op jit(solution)/shard_map/all_to_all | solution.py:136
  417.9 8.5 fusion.13
  443.0 64.0 %all-to-all-done.5 = f32[8,128,768]{2,1,0:T(8,128)S(1)} async-done(((f32[8,128,768]{2,1,0:T(8,128)}), f32[8,128,768]{2,1,0:T(8,128)S(1)}, u32[]{:S(2)}, u32[]{:S(2)}) %all-to-all-start.5) | async-done | bytes 3145760 | tf_op jit(solution)/shard_map/all_to_all | solution.py:157
  531.0 52.1 %all-to-all-done.3 = f32[8,128,768]{2,1,0:T(8,128)S(1)} async-done(((f32[8,128,768]{2,1,0:T(8,128)}), f32[8,128,768]{2,1,0:T(8,128)S(1)}, u32[]{:S(2)}, u32[]{:S(2)}) %all-to-all-start.3) | async-done | bytes 3145760 | tf_op jit(solution)/shard_map/all_to_all | solution.py:83
  591.1 8.1 multiply_reduce_fusion.3
  599.2 9.8 psum.131
  628.7 43.2 %all-reduce.25.cloned.1.call-done = f32[394,768]{1,0:T(8,128)} async-done(((f32[394,768]{1,0:T(8,128)}), f32[394,768]{1,0:T(8,128)}) %all-reduce.25.cloned.1.call-update) | async-done | bytes 1210384 | tf_op jit(solution)/shard_map/psum | solution.py:231
  682.1 8.9 scatter_custom_fusion.3
  691.0 42.5 %all_to_all.41 = bf16[8,128,768]{2,1,0:T(8,128)(2,1)S(1)} all-to-all(bf16[8,128,768]{2,1,0:T(8,128)(2,1)} %bitcast.270), channel_id=1, replica_groups=mesh['tensor'=2,'expert'=8,'replica'=2] {'expert'}, dimensions={0} | all-to-all | bytes 3145728 | tf_op jit(solution)/shard_map/all_to_all | solution.py:136
  733.5 9.1 fusion.6
  752.5 70.2 %all-to-all-done.7 = f32[8,128,768]{2,1,0:T(8,128)S(1)} async-done(((f32[8,128,768]{2,1,0:T(8,128)}), f32[8,128,768]{2,1,0:T(8,128)S(1)}, u32[]{:S(2)}, u32[]{:S(2)}) %all-to-all-start.7) | async-done | bytes 3145760 | tf_op jit(solution)/shard_map/all_to_all | solution.py:157
  842.7 14.4 %psum.134 = f32[394,2]{1,0:T(8,128)S(1)} all-reduce(f32[394,2]{1,0:T(8,128)S(1)} %multiply_reduce_fusion.2), channel_id=1, replica_groups=mesh['tensor'=2,'expert'=8,'replica'=2] {'tensor'}, use_global_device_ids=true, to_apply=%region_47.50 | all-reduce | flops 788 | bytes 6304 | tf_op jit(solution)/shard_map/psum | solution.py:162
  857.3 25.8 %all-reduce.27.cloned.1.call-done = f32[394,768]{1,0:T(8,128)} async-done(((f32[394,768]{1,0:T(8,128)}), f32[394,768]{1,0:T(8,128)}) %all-reduce.27.cloned.1.call-update) | async-done | bytes 1210384 | tf_op jit(solution)/shard_map/psum | solution.py:162
  911.8 37.3 %all-reduce.31.cloned.1.call-done = (f32[2,3,768,384]{2,3,1,0:T(8,128)}, f32[2,384,768]{2,1,0:T(8,128)}) async-done(((f32[2,3,768,384]{2,3,1,0:T(8,128)}, f32[2,384,768]{2,1,0:T(8,128)}), (f32[2,3,768,384]{2,3,1,0:T(8,128)}, f32[2,384,768]{2,1,0:T(8,128)})) %all-reduce.31.cloned.1.call-update) | async-done | bytes 9437200 | tf_op jit(solution)/shard_map/psum | solution.py:249
  976.1 47.6 %all-reduce.33.cloned.1.call-done = (f32[394,768]{1,0:T(8,128)}, f32[394,768]{1,0:T(8,128)}) async-done(((f32[394,768]{1,0:T(8,128)}, f32[394,768]{1,0:T(8,128)}), (f32[394,768]{1,0:T(8,128)}, f32[394,768]{1,0:T(8,128)})) %all-reduce.33.cloned.1.call-update) | async-done | bytes 2420752 | tf_op jit(solution)/shard_map/psum | solution.py:86
  1029.8 40.9 %all-reduce.2 = (f32[2,2,768]{2,1,0:T(2,128)}, f32[2,768,8]{1,2,0:T(8,128)}) all-reduce(f32[2,2,768]{2,1,0:T(2,128)S(1)} %get-tuple-element.68, f32[2,768,8]{1,2,0:T(8,128)S(1)} %get-tuple-element.69), channel_id=1, replica_groups=mesh['tensor'=2,'expert'=8,'replica'=2] {'expert'}, use_global_device_ids=true, to_apply=%region_61.64 | all-reduce | flops 15360 | bytes 122880 | tf_op jit(solution)/shard_map/psum | solution.py:248
  1074.1 253.6 %all-reduce.29.cloned.1.call-done = (f32[2,3,768,384]{2,3,1,0:T(8,128)}, f32[2,384,768]{2,1,0:T(8,128)}) async-done(((f32[2,3,768,384]{2,3,1,0:T(8,128)}, f32[2,384,768]{2,1,0:T(8,128)}), (f32[2,3,768,384]{2,3,1,0:T(8,128)}, f32[2,384,768]{2,1,0:T(8,128)})) %all-reduce.29.cloned.1.call-update) | async-done | bytes 9437200 | tf_op jit(solution)/shard_map/psum | solution.py:248
  1327.6 8.3 copy.267
  1335.9 11.2 reduce-scatter.5.cloned.1.call-done
  1347.2 21.9 %reduce-scatter.3.cloned.1.call-done = f32[2,384,1536]{2,1,0:T(8,128)} async-done(((f32[2,768,1536]{2,1,0:T(8,128)}), f32[2,384,1536]{2,1,0:T(8,128)}) %reduce-scatter.3.cloned.1.call-update) | async-done | bytes 4718608 | tf_op jit(solution)/shard_map/reduce_scatter | solution.py:245
  (500 shorter events, 282.8 us)
Async XLA Ops:
  7.2 61.4 %all-reduce.17.cloned.1.call-start = ((), (), s32[]{:S(2)}) async-start(), calls=%async_computation.10 | async-start | bytes 2457600 | tf_op jit(solution)/shard_map/psum | solution.py:59
  11.3 59.1 %copy-start.85 = (f32[768]{0:T(1024)}, f32[768]{0:T(1024)S(1)}, u32[]{:S(2)}) copy-start(f32[768]{0:T(1024)S(1)} %get-tuple-element.61) | copy-start | bytes 9220
  33.0 104.6 %copy-start.118 = (s32[788]{0:T(1024)}, s32[788]{0:T(1024)S(1)}, u32[]{:S(2)}) copy-start(s32[788]{0:T(1024)S(1)} %fusion.150) | copy-start | bytes 9460
  79.4 50.2 %slice-start = ((s8[4718592]{0:T(1024)(128)(4,1)}), s8[4194304]{0:T(1024)(128)(4,1)S(1)}, s32[]{:S(2)}) async-start(s8[4718592]{0:T(1024)(128)(4,1)} %bitcast.280), calls=%async_computation.21 | async-start | bytes 8388608
  133.8 74.1 %all-to-all-start.1 = ((f32[8,128,768]{2,1,0:T(8,128)}), f32[8,128,768]{2,1,0:T(8,128)S(1)}, u32[]{:S(2)}, u32[]{:S(2)}) async-start(f32[8,128,768]{2,1,0:T(8,128)} %fusion.20), calls=%async_computation.1 | async-start | bytes 6291456 | tf_op jit(solution)/shard_map/all_to_all | solution.py:83
  137.6 124.8 %all-reduce.19.cloned.1.call-start = ((), (), s32[]{:S(2)}) async-start(), calls=%async_computation.11 | async-start | bytes 2457600 | tf_op jit(solution)/shard_map/psum | solution.py:86
  137.7 70.2 %copy-start.102 = (s32[1024]{0:T(1024)}, s32[1024]{0:T(1024)S(1)}, u32[]{:S(2)}) copy-start(s32[1024]{0:T(1024)S(1)} %pad_clamp_fusion.1) | copy-start | bytes 12292
  220.2 101.4 %all-reduce.21.cloned.1.call-start = ((), (), s32[]{:S(2)}) async-start(), calls=%async_computation.12 | async-start | bytes 2457600 | tf_op jit(solution)/shard_map/psum | solution.py:59
  264.1 57.5 %copy-start.11 = (f32[394,768]{1,0:T(8,128)}, f32[394,768]{1,0:T(8,128)S(1)}, u32[]{:S(2)}) copy-start(f32[394,768]{1,0:T(8,128)S(1)} %get-tuple-element.83) | copy-start | bytes 3631108
  334.0 42.8 %all-to-all-start.2 = ((bf16[8,128,768]{2,1,0:T(8,128)(2,1)}), bf16[8,128,768]{2,1,0:T(8,128)(2,1)S(1)}, u32[]{:S(2)}, u32[]{:S(2)}) async-start(bf16[8,128,768]{2,1,0:T(8,128)(2,1)} %bitcast.268), calls=%async_computation.2 | async-start | bytes 3145728 | tf_op jit(solution)/shard_map/all_to_all | solution.py:74
  376.8 41.2 %all-to-all-start.4 = ((bf16[8,128,768]{2,1,0:T(8,128)(2,1)}), bf16[8,128,768]{2,1,0:T(8,128)(2,1)}, u32[]{:S(2)}, u32[]{:S(2)}) async-start(bf16[8,128,768]{2,1,0:T(8,128)(2,1)} %bitcast.269), calls=%async_computation.4 | async-start | bytes 3145728 | tf_op jit(solution)/shard_map/all_to_all | solution.py:136
  381.3 46.8 %slice-start.2 = ((s8[4718592]{0:T(1024)(128)(4,1)}), s8[524288]{0:T(1024)(128)(4,1)S(1)}, s32[]{:S(2)}) async-start(s8[4718592]{0:T(1024)(128)(4,1)} %bitcast.282), calls=%async_computation.23 | async-start | bytes 1048576
  432.4 74.5 %all-to-all-start.5 = ((f32[8,128,768]{2,1,0:T(8,128)}), f32[8,128,768]{2,1,0:T(8,128)S(1)}, u32[]{:S(2)}, u32[]{:S(2)}) async-start(f32[8,128,768]{2,1,0:T(8,128)} %fusion.16), calls=%async_computation.5 | async-start | bytes 6291456 | tf_op jit(solution)/shard_map/all_to_all | solution.py:157
  508.6 74.5 %all-to-all-start.3 = ((f32[8,128,768]{2,1,0:T(8,128)}), f32[8,128,768]{2,1,0:T(8,128)S(1)}, u32[]{:S(2)}, u32[]{:S(2)}) async-start(f32[8,128,768]{2,1,0:T(8,128)} %fusion.18), calls=%async_computation.3 | async-start | bytes 6291456 | tf_op jit(solution)/shard_map/all_to_all | solution.py:83
  512.2 97.0 %all-reduce.23.cloned.1.call-start = ((), (), s32[]{:S(2)}) async-start(), calls=%async_computation.13 | async-start | bytes 2457600 | tf_op jit(solution)/shard_map/psum | solution.py:162
  528.8 143.1 %all-reduce.25.cloned.1.call-start = ((), (), s32[]{:S(2)}) async-start(), calls=%async_computation.14 | async-start | bytes 2457600 | tf_op jit(solution)/shard_map/psum | solution.py:231
  625.0 46.9 %copy-start.88 = (f32[768]{0:T(1024)S(1)}, f32[768]{0:T(1024)}, u32[]{:S(2)}) copy-start(f32[768]{0:T(1024)} %get-tuple-element.63) | copy-start | bytes 9220
  625.0 46.9 %copy-start.91 = (f32[394]{0:T(512)S(1)}, f32[394]{0:T(512)}, u32[]{:S(2)}) copy-start(f32[394]{0:T(512)} %copy-done.90) | copy-start | bytes 4732
  625.0 46.9 %copy-start.105 = (f32[394]{0:T(512)S(1)}, f32[394]{0:T(512)}, u32[]{:S(2)}) copy-start(f32[394]{0:T(512)} %copy-done.104) | copy-start | bytes 4732
  628.5 45.3 %copy-start.115 = (f32[394]{0:T(512)S(1)}, f32[394]{0:T(512)}, u32[]{:S(2)}) copy-start(f32[394]{0:T(512)} %copy-done.114) | copy-start | bytes 4732
  682.1 62.2 %slice-start.4 = ((s8[4718592]{0:T(1024)(128)(4,1)}), s8[524288]{0:T(1024)(128)(4,1)S(1)}, s32[]{:S(2)}) async-start(s8[4718592]{0:T(1024)(128)(4,1)} %bitcast.284), calls=%async_computation.25 | async-start | bytes 1048576
  748.6 74.1 %copy-start.103 = (s32[1024]{0:T(1024)S(1)}, s32[1024]{0:T(1024)}, u32[]{:S(2)}) copy-start(s32[1024]{0:T(1024)} %copy-done.102) | copy-start | bytes 12292
  748.6 74.1 %all-to-all-start.7 = ((f32[8,128,768]{2,1,0:T(8,128)}), f32[8,128,768]{2,1,0:T(8,128)S(1)}, u32[]{:S(2)}, u32[]{:S(2)}) async-start(f32[8,128,768]{2,1,0:T(8,128)} %fusion.14), calls=%async_computation.7 | async-start | bytes 6291456 | tf_op jit(solution)/shard_map/all_to_all | solution.py:157
  752.4 130.7 %all-reduce.27.cloned.1.call-start = ((), (), s32[]{:S(2)}) async-start(), calls=%async_computation.15 | async-start | bytes 2457600 | tf_op jit(solution)/shard_map/psum | solution.py:162
  836.4 112.7 %all-reduce.31.cloned.1.call-start = ((), (), s32[]{:S(2)}) async-start(), calls=%async_computation.19 | async-start | bytes 18874368 | tf_op jit(solution)/shard_map/psum | solution.py:249
  908.2 115.5 %all-reduce.33.cloned.1.call-start = ((), (), s32[]{:S(2)}) async-start(), calls=%async_computation.20 | async-start | bytes 4915200 | tf_op jit(solution)/shard_map/psum | solution.py:86
  911.8 415.9 %all-reduce.29.cloned.1.call-start = ((), (), s32[]{:S(2)}) async-start(), calls=%async_computation.18 | async-start | bytes 18874368 | tf_op jit(solution)/shard_map/psum | solution.py:248
  949.2 398.0 %reduce-scatter.5.cloned.1.call-start = ((), (), s32[]{:S(2)}) async-start(), calls=%async_computation.17 | async-start | bytes 14155776 | tf_op jit(solution)/shard_map/reduce_scatter | solution.py:246
  962.0 407.1 %reduce-scatter.3.cloned.1.call-start = ((), (), s32[]{:S(2)}) async-start(), calls=%async_computation.16 | async-start | bytes 14155776 | tf_op jit(solution)/shard_map/reduce_scatter | solution.py:245
  975.7 49.8 %copy-start.111 = (f32[394]{0:T(512)S(1)}, f32[394]{0:T(512)}, u32[]{:S(2)}) copy-start(f32[394]{0:T(512)} %copy-done.110) | copy-start | bytes 4732
  1023.7 47.0 %copy-start.7 = (f32[394,768]{1,0:T(8,128)S(1)}, f32[394,768]{1,0:T(8,128)}, u32[]{:S(2)}) copy-start(f32[394,768]{1,0:T(8,128)} %copy-done.5) | copy-start | bytes 3631108
  1023.7 47.0 %copy-start.21 = (f32[394,768]{1,0:T(8,128)S(1)}, f32[394,768]{1,0:T(8,128)}, u32[]{:S(2)}) copy-start(f32[394,768]{1,0:T(8,128)} %copy-done.20) | copy-start | bytes 3631108
  (114 other events, 828.9 us)
Sparse Core Ops, SparseCore 0:
  21.8 46.6 all-reduce.16
  220.3 42.0 all-reduce.18
  277.6 43.9 all-reduce.20
  528.9 44.3 all-reduce.22
  628.7 43.1 all-reduce.24
  836.6 46.4 all-reduce.26
  908.3 40.7 all-reduce.30
  951.5 72.1 all-reduce.32
  1027.7 299.8 all-reduce.28
  1330.4 16.7 reduce-scatter.4
  1350.0 19.0 reduce-scatter.2
